TPU v7x, 256 devices: a whole 4x4x8 slice. The times are simulated.
256 devices in a mesh: row: 16 (over x, y_hi, core), col: 16 (over y_lo, z).
Axes of the slice: x: 4, y: 4 (y_hi: 2, y_lo: 2; y = y_hi * 2 + y_lo), z: 8, core: 2. Of those that a mesh axis runs over, the one named last changes fastest.
Arguments:
- specimen_transmit: float32 [2, 2, 4096, 4096], P(None, None, 'row', 'col'), may hold values from -5 to 5
- illumination: float32 [2, 256, 256], replicated, may hold values from -5 to 5
- fresnel_angle: float32 [256, 256], replicated, may hold values from -3.140625 to 3.140625
- recorded_intensity: float32 [16, 16, 2, 256, 256], P('row', 'col'), may hold values from 0.1 to 3
- frame_shifts: int32 [16, 16, 2, 2], P('row', 'col'), may hold values from -128 to 128, as said below
Outputs:
- obj_grad: float32 [2, 2, 4096, 4096], P(None, None, 'row', 'col')
- probe_grad: float32 [2, 256, 256], P(None, 'row', 'col')
Inputs may be any that keep to these rules, and one draw needn't show every extreme that they name: `frame_shifts`: shifts stay within the margin, so a window reaches only its own tile and the eight tiles around it; both ends of the range occur in every draw.
All inputs are finite; a program needn't handle non-finite values.
Results may differ from a plain program's by a relative error of at most 0.0003.
Values sent between devices are 32-bit elements; how exact they have to be, the bound alone decides.
No kernel may reach another device: no remote copies, remote signals or barrier semaphores. Data moves between devices by JAX's collectives and lax.ppermute only.
A program may use at most 128 MiB of HBM per device.

v0:
```python
import math

import jax
import jax.numpy as jnp
import numpy as np
from jax import lax
from jax.experimental import pallas as pl
from jax.experimental.pallas import tpu as pltpu
from jax.sharding import PartitionSpec as P


HALO = 128
TILE = 256
SIDE = TILE + 2 * HALO
PARTS = 4
F32 = jnp.float32
BF16 = jnp.bfloat16


def half_tables():
    n = np.arange(128)[:, None]
    out = []
    for odd in (0, 1):
        k = 2 * np.arange(128)[None, :] + odd
        angle = 2.0 * math.pi * ((n * k) % TILE) / TILE
        c, s = np.cos(angle) / 16.0, np.sin(angle) / 16.0
        whole = np.block([[c, -s], [s, c]]).astype(np.float32)
        for m in (whole, whole.T):
            high = m.astype(jnp.bfloat16)
            low = (m - high.astype(np.float32)).astype(jnp.bfloat16)
            out += [high, low]
    return np.stack(out)


EVEN, EVEN_T, ODD, ODD_T = 0, 2, 4, 6


def two(x):
    high = x.astype(BF16)
    return high, (x - high.astype(F32)).astype(BF16)


def dot(a, b):
    return jnp.dot(a, b, preferred_element_type=F32)


def right(x, tables, which):
    high, low = two(x)
    t, tl = tables[which], tables[which + 1]
    return dot(lanes(high, low, high), rows(t, t, tl))


def left(tables, which, x):
    high, low = two(x)
    t, tl = tables[which], tables[which + 1]
    return dot(lanes(t, t, tl), rows(high, low, high))


def rows(*parts):
    return jnp.concatenate(parts, axis=0)


def lanes(*parts):
    return jnp.concatenate(parts, axis=1)


def forward(re, im, tables):
    a = lanes(re[:, :128] + re[:, 128:], im[:, :128] + im[:, 128:])
    b = lanes(re[:, :128] - re[:, 128:], im[:, :128] - im[:, 128:])
    e = right(a, tables, EVEN)
    o = right(b, tables, ODD)
    pe, po = e[:128] + e[128:], o[:128] + o[128:]
    qe, qo = e[:128] - e[128:], o[:128] - o[128:]
    p = rows(lanes(pe[:, :128], po[:, :128]), lanes(pe[:, 128:], po[:, 128:]))
    q = rows(lanes(qe[:, :128], qo[:, :128]), lanes(qe[:, 128:], qo[:, 128:]))
    fe = left(tables, EVEN_T, p)
    fo = left(tables, ODD_T, q)
    return rows(fe[:128], fo[:128]), rows(fe[128:], fo[128:])


def inverse(re, im, tables):
    p = left(tables, EVEN, rows(re[:128], im[:128]))
    q = left(tables, ODD, rows(re[128:], im[128:]))
    top, bottom = p + q, p - q
    sr, si = rows(top[:128], bottom[:128]), rows(top[128:], bottom[128:])
    p = right(lanes(sr[:, :128], si[:, :128]), tables, EVEN_T)
    q = right(lanes(sr[:, 128:], si[:, 128:]), tables, ODD_T)
    u, v = p + q, p - q
    return lanes(u[:, :128], v[:, :128]), lanes(u[:, 128:], v[:, 128:])


def complex_product(a_real, a_imag, b_real, b_imag):
    return (a_real * b_real - a_imag * b_imag, a_real * b_imag + a_imag * b_real)


def conj_product(a_real, a_imag, b_real, b_imag):
    return (a_real * b_real + a_imag * b_imag, a_real * b_imag - a_imag * b_real)


OUTER, INNER, SIDE_A, SIDE_B = 0, 1, 2, 3


def at(where, which, back=0):
    return pl.multiple_of(where[which] - back, 128)


def pack_kernel(where, x, outer, side_a, side_b):
    outer[...] = x[:, pl.ds(pl.multiple_of(where[OUTER] // 3, 128), HALO), :]
    side_a[...] = x[:, :, pl.ds(pl.multiple_of(where[SIDE_A] // 3, 128), HALO)]
    side_b[...] = x[:, :, pl.ds(pl.multiple_of(where[SIDE_B] // 3, 128), HALO)]


def corner_kernel(where, outer, corner_a):
    corner_a[...] = outer[:, :, pl.ds(pl.multiple_of(where[SIDE_A] // 3, 128), HALO)]


def inner_kernel(where, x, got_a, got_b, inner, corner_b):
    edge = pl.ds(pl.multiple_of(where[INNER] // 3, 128), HALO)
    inner[:, :, :TILE] = x[:, edge, :]
    inner[:, :, TILE : TILE + HALO] = got_a[:, edge, :]
    inner[:, :, TILE + HALO :] = got_b[:, edge, :]
    corner_b[...] = got_b[:, pl.ds(pl.multiple_of(where[OUTER] // 3, 128), HALO), :]


def prepare_kernel(inphase, quadrature, intensity, out):
    i = lax.broadcasted_iota(jnp.int32, (TILE, TILE), 0)
    j = lax.broadcasted_iota(jnp.int32, (TILE, TILE), 1)
    pick = (i == jnp.where(j < 128, 2 * j, 2 * j - 255)).astype(F32)
    turn = (j == jnp.where(i < 128, 2 * i, 2 * i - 255)).astype(F32)

    def sort(x):
        x = jnp.dot(x, pick, precision=lax.Precision.HIGHEST, preferred_element_type=F32)
        return jnp.dot(turn, x, precision=lax.Precision.HIGHEST, preferred_element_type=F32)

    out[0] = sort(inphase[...])
    out[1] = sort(quadrature[...])
    out[2] = sort(intensity[0])
    out[3] = sort(intensity[1])


def main_kernel(
    where, shifts, x, outer, got_a, got_b, corner_a, corner_b, inner, probe, sorted_, tables,
    g_own, g_outer, g_a, g_b, g_corner_a, g_corner_b, g_inner, probe_out,
    ext, acc,
):
    own = pl.ds(HALO, TILE)
    o, i = pl.ds(at(where, OUTER), HALO), pl.ds(at(where, INNER), HALO)
    a, b = pl.ds(at(where, SIDE_A), HALO), pl.ds(at(where, SIDE_B), HALO)
    ext[:, own, own] = x[...]
    ext[:, o, own] = outer[...]
    ext[:, own, a] = got_a[...]
    ext[:, own, b] = got_b[...]
    ext[:, o, a] = corner_a[...]
    ext[:, o, b] = corner_b[...]
    ext[:, i, own] = inner[:, :, :TILE]
    ext[:, i, a] = inner[:, :, TILE : TILE + HALO]
    ext[:, i, b] = inner[:, :, TILE + HALO :]
    acc[...] = jnp.zeros_like(acc)
    filter_r, filter_i = sorted_[0], sorted_[1]
    probe_r, probe_i = probe[0], probe[1]
    places, turns, steps = [], [], []
    for p in range(2):
        start_row = shifts[0, 0, p, 0] + HALO
        start_col = shifts[0, 0, p, 1] + HALO
        turn, step = lax.rem(start_col, 128), lax.rem(start_row, 8)
        turns.append(turn)
        steps.append(step)
        places.append(
            (
                pl.ds(pl.multiple_of(start_row - step, 8), TILE + 8),
                pl.ds(pl.multiple_of(start_col - turn, 128), TILE + HALO),
            )
        )

    def window(p, part):
        wide = ext[(part, *places[p])]
        wide = pltpu.roll(wide, lax.rem(TILE + HALO - turns[p], TILE + HALO), 1)[:, :TILE]
        return pltpu.roll(wide, lax.rem(TILE + 8 - steps[p], TILE + 8), 0)[:TILE]

    def add(p, part, value):
        wide = lanes(value, jnp.zeros((TILE, HALO), F32))
        wide = pltpu.roll(wide, turns[p], 1)
        wide = rows(wide, jnp.zeros((8, TILE + HALO), F32))
        acc[(part, *places[p])] += pltpu.roll(wide, steps[p], 0)

    both = (0, 1)
    x0 = [(window(p, 0), window(p, 1)) for p in both]
    e0 = [complex_product(probe_r, probe_i, *x0[p]) for p in both]
    spec = [complex_product(*forward(*e0[p], tables), filter_r, filter_i) for p in both]
    psi = [inverse(*spec[p], tables) for p in both]
    x1 = [(window(p, 2), window(p, 3)) for p in both]
    e1 = [complex_product(*psi[p], *x1[p]) for p in both]
    far = [forward(*e1[p], tables) for p in both]
    back = []
    for p in both:
        far_r, far_i = far[p]
        misfit = far_r * far_r + far_i * far_i - sorted_[2 + p]
        back.append(inverse(misfit * far_r, misfit * far_i, tables))
    for p in both:
        for part, value in enumerate(conj_product(*psi[p], *back[p])):
            add(p, 2 + part, value)
    h1 = [conj_product(*x1[p], *back[p]) for p in both]
    spec = [conj_product(filter_r, filter_i, *forward(*h1[p], tables)) for p in both]
    back = [inverse(*spec[p], tables) for p in both]
    for p in both:
        for part, value in enumerate(conj_product(probe_r, probe_i, *back[p])):
            add(p, part, value)
    h0 = [conj_product(*x0[p], *back[p]) for p in both]
    total = h0[0][0] + h0[1][0], h0[0][1] + h0[1][1]
    for k in range(16):
        for part in range(2):
            probe_out[k, part] = total[part][16 * k : 16 * k + 16]
    g_own[...] = acc[:, own, own]
    g_outer[...] = acc[:, o, own]
    g_a[...] = acc[:, own, a]
    g_b[...] = acc[:, own, b]
    g_corner_a[...] = acc[:, o, a]
    g_corner_b[...] = acc[:, o, b]
    g_inner[:, :, :TILE] = acc[:, i, own]
    g_inner[:, :, TILE : TILE + HALO] = acc[:, i, a]
    g_inner[:, :, TILE + HALO :] = acc[:, i, b]


def sides_kernel(where, g_a, g_b, inner, side_a, side_b):
    edge = pl.ds(pl.multiple_of(where[INNER] // 3, 128), HALO)
    side_a[...] = g_a[...]
    side_b[...] = g_b[...]
    side_a[:, edge, :] += inner[:, :, TILE : TILE + HALO]
    side_b[:, edge, :] += inner[:, :, TILE + HALO :]


def outer_kernel(where, outer, corner_a, corner_b, out):
    out[...] = outer[...]
    out[:, :, pl.ds(pl.multiple_of(where[SIDE_A] // 3, 128), HALO)] += corner_a[...]
    out[:, :, pl.ds(pl.multiple_of(where[SIDE_B] // 3, 128), HALO)] += corner_b[...]


def final_kernel(where, own, inner, side_a, side_b, outer, out):
    out[...] = own[...]
    out[:, pl.ds(pl.multiple_of(where[INNER] // 3, 128), HALO), :] += inner[:, :, :TILE]
    out[:, :, pl.ds(pl.multiple_of(where[SIDE_A] // 3, 128), HALO)] += side_a[...]
    out[:, :, pl.ds(pl.multiple_of(where[SIDE_B] // 3, 128), HALO)] += side_b[...]
    out[:, pl.ds(pl.multiple_of(where[OUTER] // 3, 128), HALO), :] += outer[...]


def strip_kernel(got, out):
    total = got[0]
    for k in range(1, 16):
        total = total + got[k]
    tall = rows(total[0], total[1], jnp.zeros((96, TILE), F32)).T
    for k in range(16):
        quads = [tall[16 * k + 4 * j : 16 * k + 4 * j + 4, :32] for j in range(4)]
        out[k] = lanes(*quads)


def patch_kernel(got, out):
    total = got[0]
    for k in range(1, 16):
        total = total + got[k]
    quads = [total[:, 32 * j : 32 * j + 32] for j in range(4)]
    wide = lanes(rows(*quads), jnp.zeros((16, 96), F32))
    tall = rows(wide, jnp.zeros((112, 128), F32)).T
    out[0] = tall[:16, :16]
    out[1] = tall[16:32, :16]


def call(kernel, shapes, *operands, scalars=1, scratch=(), flops=0, grant=6, hbm=False):
    smem = pl.BlockSpec(memory_space=pltpu.SMEM)
    vmem = pl.BlockSpec(memory_space=pltpu.VMEM)
    specs = [smem if k < scalars else vmem for k in range(len(operands))]
    size = sum(4 * math.prod(s) for s in shapes)
    return pl.pallas_call(
        kernel,
        out_shape=[pltpu.HBM(s, F32) if hbm else jax.ShapeDtypeStruct(s, F32) for s in shapes],
        in_specs=specs,
        out_specs=[vmem] * len(shapes),
        scratch_shapes=list(scratch),
        cost_estimate=pl.CostEstimate(flops=flops, bytes_accessed=2 * size, transcendentals=0),
        compiler_params=pltpu.CompilerParams(vmem_limit_bytes=grant * 1024 * 1024),
    )(*operands)


NEAR = [(i, i ^ 1) for i in range(16)]
FAR = [(i, (i - 1 if i % 2 == 0 else i + 1) % 16) for i in range(16)]


def body(specimen_transmit, illumination, fresnel_angle, recorded_intensity, frame_shifts):
    row_odd = lax.axis_index("row") % 2
    col_odd = lax.axis_index("col") % 2
    outer_at, side_b_at = 384 * row_odd, 384 * col_odd
    where = jnp.stack([outer_at, 384 - outer_at, 384 - side_b_at, side_b_at]).astype(jnp.int32)
    x = specimen_transmit.reshape(PARTS, TILE, TILE)
    row_strip, col_strip = (PARTS, HALO, TILE), (PARTS, TILE, HALO)
    corner, wide_strip = (PARTS, HALO, HALO), (PARTS, HALO, SIDE)

    outer, side_a, side_b = call(pack_kernel, [row_strip, col_strip, col_strip], where, x)
    outer = lax.ppermute(outer, "row", FAR)
    got_b = lax.ppermute(side_b, "col", FAR)
    got_a = lax.ppermute(side_a, "col", NEAR)
    (ordered,) = call(
        prepare_kernel, [(4, TILE, TILE)],
        jnp.cos(fresnel_angle), jnp.sin(fresnel_angle), recorded_intensity[0, 0],
        scalars=0, flops=300_000_000,
    )
    (corner_a,) = call(corner_kernel, [corner], where, outer)
    corner_a = lax.ppermute(corner_a, "col", NEAR)
    inner, corner_b = call(inner_kernel, [wide_strip, corner], where, x, got_a, got_b)
    corner_b = lax.ppermute(corner_b, "row", FAR)
    inner = lax.ppermute(inner, "row", NEAR)

    tables = jnp.asarray(half_tables())
    own, outer, side_a, side_b, corner_a, corner_b, inner, probe = call(
        main_kernel,
        [(PARTS, TILE, TILE), row_strip, col_strip, col_strip, corner, corner, wide_strip,
         (16, 2, 16, TILE)],
        where, frame_shifts, x, outer, got_a, got_b, corner_a, corner_b, inner, illumination,
        ordered, tables, scalars=2,
        scratch=[pltpu.VMEM((PARTS, SIDE + 8, SIDE + HALO), F32)] * 2, flops=5_000_000_000, grant=26,
        hbm=True,
    )

    inner = lax.ppermute(inner, "row", NEAR)
    corner_b = lax.ppermute(corner_b, "col", FAR)
    corner_a = lax.ppermute(corner_a, "col", NEAR)
    side_a, side_b = call(sides_kernel, [col_strip] * 2, where, side_a, side_b, inner)
    side_a = lax.ppermute(side_a, "col", NEAR)
    side_b = lax.ppermute(side_b, "col", FAR)
    (outer,) = call(outer_kernel, [row_strip], where, outer, corner_a, corner_b)
    outer = lax.ppermute(outer, "row", FAR)
    (result,) = call(final_kernel, [(PARTS, TILE, TILE)], where, own, inner, side_a, side_b, outer)

    probe = lax.all_to_all(probe, "row", 0, 0, tiled=True)
    (probe,) = call(strip_kernel, [(16, 4, 128)], probe, scalars=0, grant=4)
    probe = lax.all_to_all(probe, "col", 0, 0, tiled=True)
    (probe,) = call(patch_kernel, [(2, 16, 16)], probe, scalars=0, grant=4)
    return (result.reshape(specimen_transmit.shape), probe)


def solution(mesh):
    placed = (
        P(None, None, "row", "col"),
        P(),
        P(),
        P("row", "col", None, None, None),
        P("row", "col", None, None),
    )
    return jax.shard_map(
        body,
        mesh=mesh,
        in_specs=placed,
        out_specs=(P(None, None, "row", "col"), P(None, "row", "col")),
        check_vma=False,
    )
```

profile of v0, /device:TPU:6, one launch (start us, length us, event | category | flops | bytes accessed | tf_op | source)
XLA Modules:
  0.0 116.5 jit_solution(9894489987028223738)
XLA Ops:
  0.6 0.1 pad_add_fusion.where
  0.7 1.2 %copy-done = f32[2,2,256,256]{3,2,1,0:T(8,128)S(1)} copy-done((f32[2,2,256,256]{3,2,1,0:T(8,128)S(1)}, f32[2,2,256,256]{3,2,1,0:T(8,128)}, u32[]{:S(2)}) %copy-start) | copy-done | bytes 1048600
  2.0 0.7 shard_map.77
  2.6 2.0 %collective-permute-start.1 = (f32[4,256,128]{2,1,0:T(8,128)S(1)}, f32[4,256,128]{2,1,0:T(8,128)S(1)}, u32[]{:S(2)}, u32[]{:S(2)}) collective-permute-start(f32[4,256,128]{2,1,0:T(8,128)S(1)} %get-tuple-element.18), channel_id=1, source_target_pairs={{0,1},{1,0},{2,3},{3,2},{4,5},{5,4},{6,7},{7,6},{8,9},{9,8},{10,11... | collective-permute-start | bytes 1572872 | tf_op jit(solution)/shard_map/ppermute | solution.py:299
  4.6 6.0 %collective-permute-start.2 = (f32[4,256,128]{2,1,0:T(8,128)S(1)}, f32[4,256,128]{2,1,0:T(8,128)S(1)}, u32[]{:S(2)}, u32[]{:S(2)}) collective-permute-start(f32[4,256,128]{2,1,0:T(8,128)S(1)} %get-tuple-element.19), channel_id=1, source_target_pairs={{0,15},{1,2},{2,1},{3,4},{4,3},{5,6},{6,5},{7,8},{8,7},{9,10},{10,... | collective-permute-start | bytes 1572872 | tf_op jit(solution)/shard_map/ppermute | solution.py:298
  10.6 6.0 %collective-permute-done.1.got_a = f32[4,256,128]{2,1,0:T(8,128)S(1)} collective-permute-done((f32[4,256,128]{2,1,0:T(8,128)S(1)}, f32[4,256,128]{2,1,0:T(8,128)S(1)}, u32[]{:S(2)}, u32[]{:S(2)}) %collective-permute-start.1) | collective-permute-done | bytes 524320 | tf_op jit(solution)/shard_map/ppermute | solution.py:299
  16.5 5.7 %collective-permute-done.2.got_b = f32[4,256,128]{2,1,0:T(8,128)S(1)} collective-permute-done((f32[4,256,128]{2,1,0:T(8,128)S(1)}, f32[4,256,128]{2,1,0:T(8,128)S(1)}, u32[]{:S(2)}, u32[]{:S(2)}) %collective-permute-start.2) | collective-permute-done | bytes 524320 | tf_op jit(solution)/shard_map/ppermute | solution.py:298
  22.2 0.7 shard_map.79
  22.9 0.1 collective-permute-start.5
  23.0 3.3 %collective-permute-start = (f32[4,128,256]{2,1,0:T(8,128)S(1)}, f32[4,128,256]{2,1,0:T(8,128)S(1)}, u32[]{:S(2)}, u32[]{:S(2)}) collective-permute-start(f32[4,128,256]{2,1,0:T(8,128)S(1)} %get-tuple-element.17), channel_id=1, source_target_pairs={{0,240},{16,32},{32,16},{48,64},{64,48},{80,96},{96,80},{112,128},... | collective-permute-start | bytes 1572872 | tf_op jit(solution)/shard_map/ppermute | solution.py:297
  26.3 7.9 %collective-permute-done.outer = f32[4,128,256]{2,1,0:T(8,128)S(1)} collective-permute-done((f32[4,128,256]{2,1,0:T(8,128)S(1)}, f32[4,128,256]{2,1,0:T(8,128)S(1)}, u32[]{:S(2)}, u32[]{:S(2)}) %collective-permute-start) | collective-permute-done | bytes 524320 | tf_op jit(solution)/shard_map/ppermute | solution.py:297
  34.2 0.6 shard_map.78
  34.8 0.0 copy-start.6
  34.8 0.1 collective-permute-start.3
  34.9 3.3 %collective-permute-start.4 = (f32[4,128,128]{2,1,0:T(8,128)S(1)}, f32[4,128,128]{2,1,0:T(8,128)S(1)}, u32[]{:S(2)}, u32[]{:S(2)}) collective-permute-start(f32[4,128,128]{2,1,0:T(8,128)S(1)} %get-tuple-element.20), channel_id=1, source_target_pairs={{0,240},{16,32},{32,16},{48,64},{64,48},{80,96},{96,80},{112,128},... | collective-permute-start | bytes 786440 | tf_op jit(solution)/shard_map/ppermute | solution.py:308
  38.2 0.0 copy-done.10
  38.2 1.1 fusion
  39.3 0.0 copy-start.1
  39.3 0.0 copy-start.7
  39.3 0.0 copy-start.8
  39.4 2.4 %shard_map.80.sorted_ = f32[4,256,256]{2,1,0:T(8,128)S(1)} custom-call(f32[256,256]{1,0:T(8,128)S(1)} %get-tuple-element.33.inphase, f32[256,256]{1,0:T(8,128)S(1)} %get-tuple-element.32.quadrature, f32[2,256,256]{2,1,0:T(8,128)S(1)} %bitcast.10), custom_call_target="tpu_custom_call" | custom-call | flops 300000000 | bytes 2097152 | tf_op jit(solution)/shard_map/pallas_call | solution.py:272
  41.7 0.0 collective-permute-done.3.corner_a
  41.7 1.5 %collective-permute-done.4.corner_b = f32[4,128,128]{2,1,0:T(8,128)S(1)} collective-permute-done((f32[4,128,128]{2,1,0:T(8,128)S(1)}, f32[4,128,128]{2,1,0:T(8,128)S(1)}, u32[]{:S(2)}, u32[]{:S(2)}) %collective-permute-start.4) | collective-permute-done | bytes 262176 | tf_op jit(solution)/shard_map/ppermute | solution.py:308
  43.2 0.0 collective-permute-done.5.inner
  43.2 0.0 copy-done.1
  43.2 14.2 %shard_map.81 = (f32[4,256,256]{2,1,0:T(8,128)}, f32[4,128,256]{2,1,0:T(8,128)}, f32[4,256,128]{2,1,0:T(8,128)}, f32[4,256,128]{2,1,0:T(8,128)}, f32[4,128,128]{...) custom-call(s32[4]{0:T(128)S(1)} %pad_add_fusion.where, ...), custom_call_target="tpu_custom_call" | custom-call | flops 5000000000 | bytes 9437184 | tf_op jit(solution)/shard_map/pallas_call | solution.py:272
  57.4 4.8 %collective-permute-start.6 = (f32[4,128,512]{2,1,0:T(8,128)}, f32[4,128,512]{2,1,0:T(8,128)S(1)}, u32[]{:S(2)}, u32[]{:S(2)}) collective-permute-start(f32[4,128,512]{2,1,0:T(8,128)} %get-tuple-element.23), channel_id=1, source_target_pairs={{0,16},{16,0},{32,48},{48,32},{64,80},{80,64},{96,112},{112,96},{1... | collective-permute-start | bytes 3145736 | tf_op jit(solution)/shard_map/ppermute | solution.py:322
  62.2 1.7 %collective-permute-start.9 = (f32[4,128,128]{2,1,0:T(8,128)}, f32[4,128,128]{2,1,0:T(8,128)S(1)}, u32[]{:S(2)}, u32[]{:S(2)}) collective-permute-start(f32[4,128,128]{2,1,0:T(8,128)} %get-tuple-element.29), channel_id=1, source_target_pairs={{0,1},{1,0},{2,3},{3,2},{4,5},{5,4},{6,7},{7,6},{8,9},{9,8},{10,11... | collective-permute-start | bytes 786440 | tf_op jit(solution)/shard_map/ppermute | solution.py:324
  63.9 3.2 %collective-permute-start.10 = (f32[4,128,128]{2,1,0:T(8,128)}, f32[4,128,128]{2,1,0:T(8,128)S(1)}, u32[]{:S(2)}, u32[]{:S(2)}) collective-permute-start(f32[4,128,128]{2,1,0:T(8,128)} %get-tuple-element.30), channel_id=1, source_target_pairs={{0,15},{1,2},{2,1},{3,4},{4,3},{5,6},{6,5},{7,8},{8,7},{9,10},{10,... | collective-permute-start | bytes 786440 | tf_op jit(solution)/shard_map/ppermute | solution.py:323
  67.1 8.6 %all-to-all-start = ((f32[16,2,16,256]{3,2,1,0:T(8,128)}), f32[16,2,16,256]{3,2,1,0:T(8,128)S(1)}, u32[]{:S(2)}, u32[]{:S(2)}) async-start(f32[16,2,16,256]{3,2,1,0:T(8,128)} %get-tuple-element.31), calls=%async_computation | async-start | bytes 1048576 | tf_op jit(solution)/shard_map/all_to_all | solution.py:332
  75.7 0.0 collective-permute-done.9.corner_a
  75.7 0.0 collective-permute-done.10.corner_b
  75.8 1.4 %shard_map.83 = f32[4,128,256]{2,1,0:T(8,128)} custom-call(s32[4]{0:T(128)S(1)} %pad_add_fusion.where, f32[4,128,256]{2,1,0:T(8,128)S(1)} %copy-done.5, f32[4,128,128]{2,1,0:T(8,128)S(1)} %collective-permute-done.9.corner_a, f32[4,128,128]{2,1,0:T(8,128)S(1)} %collective-permute-done.10.corner_b), custom_call_target="tpu_custom_call" | custom-call | bytes 1048576 | tf_op jit(solution)/shard_map/pallas_call | solution.py:272
  77.2 3.0 %collective-permute-start.11 = (f32[4,128,256]{2,1,0:T(8,128)}, f32[4,128,256]{2,1,0:T(8,128)S(1)}, u32[]{:S(2)}, u32[]{:S(2)}) collective-permute-start(f32[4,128,256]{2,1,0:T(8,128)} %shard_map.83), channel_id=1, source_target_pairs={{0,240},{16,32},{32,16},{48,64},{64,48},{80,96},{96,80},{112,128},... | collective-permute-start | bytes 1572872 | tf_op jit(solution)/shard_map/ppermute | solution.py:329
  80.2 0.0 collective-permute-done.6.inner
  80.2 0.0 copy-done.4
  80.2 0.0 copy-start.2
  80.2 1.7 %shard_map.82 = (f32[4,256,128]{2,1,0:T(8,128)}, f32[4,256,128]{2,1,0:T(8,128)}) custom-call(s32[4]{0:T(128)S(1)} %pad_add_fusion.where, f32[4,256,128]{2,1,0:T(8,128)S(1)} %copy-done.3, f32[4,256,128]{2,1,0:T(8,128)S(1)} %copy-done.4, f32[4,128,512]{2,1,0:T(8,128)S(1)} %collective-permute-done.6.inner), custom_call_target="tpu_custom_call" | custom-call | bytes 2097152 | tf_op jit(solution)/shard_map/pallas_call | solution.py:272
  81.9 0.0 collective-permute-start.7
  81.9 0.4 collective-permute-start.8
  82.3 4.7 %all-to-all-done.got = f32[16,2,16,256]{3,2,1,0:T(8,128)S(1)} async-done(((f32[16,2,16,256]{3,2,1,0:T(8,128)}), f32[16,2,16,256]{3,2,1,0:T(8,128)S(1)}, u32[]{:S(2)}, u32[]{:S(2)}) %all-to-all-start) | async-done | bytes 524320 | tf_op jit(solution)/shard_map/all_to_all | solution.py:332
  87.0 0.2 shard_map.85
  87.3 26.0 %all_to_all.10.got = f32[16,4,128]{2,1,0:T(4,128)S(1)} all-to-all(f32[16,4,128]{2,1,0:T(4,128)S(1)} %shard_map.85), channel_id=1, replica_groups=mesh['row'=16,'col'=16] {'col'}, dimensions={0} | all-to-all | bytes 65536 | tf_op jit(solution)/shard_map/all_to_all | solution.py:334
  113.2 0.8 shard_map.86
  114.0 0.0 collective-permute-done.11.outer
  114.0 0.0 collective-permute-done.7.side_a
  114.0 0.0 collective-permute-done.8.side_b
  114.0 2.5 %shard_map.84 = f32[4,256,256]{2,1,0:T(8,128)} custom-call(s32[4]{0:T(128)S(1)} %pad_add_fusion.where, f32[4,256,256]{2,1,0:T(8,128)S(1)} %copy-done.2, f32[4,128,512]{2,1,0:T(8,128)S(1)} %collective-permute-done.6.inner, f32[4,256,128]{2,1,0:T(8,128)} %collective-permute-done.7.side_a, f32[4,256,128]{2,1,0:T(8,128)} %collective-permute-done.8.side_b, ...), custom_call_target="tpu_custom_call" | custom-call | bytes 2097152 | tf_op jit(solution)/shard_map/pallas_call | solution.py:272
  (13 shorter events, 0.0 us)
Async XLA Ops:
  0.7 1.2 %copy-start = (f32[2,2,256,256]{3,2,1,0:T(8,128)S(1)}, f32[2,2,256,256]{3,2,1,0:T(8,128)}, u32[]{:S(2)}) copy-start(f32[2,2,256,256]{3,2,1,0:T(8,128)} %param.6) | copy-start | bytes 3145732
  2.6 13.9 %collective-permute-start.1 = (f32[4,256,128]{2,1,0:T(8,128)S(1)}, f32[4,256,128]{2,1,0:T(8,128)S(1)}, u32[]{:S(2)}, u32[]{:S(2)}) collective-permute-start(f32[4,256,128]{2,1,0:T(8,128)S(1)} %get-tuple-element.18), channel_id=1, source_target_pairs={{0,1},{1,0},{2,3},{3,2},{4,5},{5,4},{6,7},{7,6},{8,9},{9,8},{10,11... | collective-permute-start | bytes 1572872 | tf_op jit(solution)/shard_map/ppermute | solution.py:299
  4.6 17.6 %collective-permute-start.2 = (f32[4,256,128]{2,1,0:T(8,128)S(1)}, f32[4,256,128]{2,1,0:T(8,128)S(1)}, u32[]{:S(2)}, u32[]{:S(2)}) collective-permute-start(f32[4,256,128]{2,1,0:T(8,128)S(1)} %get-tuple-element.19), channel_id=1, source_target_pairs={{0,15},{1,2},{2,1},{3,4},{4,3},{5,6},{6,5},{7,8},{8,7},{9,10},{10,... | collective-permute-start | bytes 1572872 | tf_op jit(solution)/shard_map/ppermute | solution.py:298
  22.2 16.0 %copy-start.10 = (f32[256,256]{1,0:T(8,128)S(1)}, f32[256,256]{1,0:T(8,128)}, u32[]{:S(2)}) copy-start(f32[256,256]{1,0:T(8,128)} %param.8) | copy-start | bytes 786436
  22.9 20.3 %collective-permute-start.5 = (f32[4,128,512]{2,1,0:T(8,128)S(1)}, f32[4,128,512]{2,1,0:T(8,128)S(1)}, u32[]{:S(2)}, u32[]{:S(2)}) collective-permute-start(f32[4,128,512]{2,1,0:T(8,128)S(1)} %get-tuple-element.21), channel_id=1, source_target_pairs={{0,16},{16,0},{32,48},{48,32},{64,80},{80,64},{96,112},{112,96},{1... | collective-permute-start | bytes 3145736 | tf_op jit(solution)/shard_map/ppermute | solution.py:309
  23.0 11.2 %collective-permute-start = (f32[4,128,256]{2,1,0:T(8,128)S(1)}, f32[4,128,256]{2,1,0:T(8,128)S(1)}, u32[]{:S(2)}, u32[]{:S(2)}) collective-permute-start(f32[4,128,256]{2,1,0:T(8,128)S(1)} %get-tuple-element.17), channel_id=1, source_target_pairs={{0,240},{16,32},{32,16},{48,64},{64,48},{80,96},{96,80},{112,128},... | collective-permute-start | bytes 1572872 | tf_op jit(solution)/shard_map/ppermute | solution.py:297
  34.2 9.0 %copy-start.9 = (bf16[8,256,256]{2,1,0:T(8,128)(2,1)S(1)}, bf16[8,256,256]{2,1,0:T(8,128)(2,1)}, u32[]{:S(2)}) copy-start(bf16[8,256,256]{2,1,0:T(8,128)(2,1)} %constant.28.clone.tables) | copy-start | bytes 3145732
  34.8 4.5 %copy-start.6 = (f32[1,1,2,256,256]{4,3,2,1,0:T(8,128)S(1)}, f32[1,1,2,256,256]{4,3,2,1,0:T(8,128)}, u32[]{:S(2)}) copy-start(f32[1,1,2,256,256]{4,3,2,1,0:T(8,128)} %param.9) | copy-start | bytes 1572868
  34.8 6.9 %collective-permute-start.3 = (f32[4,128,128]{2,1,0:T(8,128)S(1)}, f32[4,128,128]{2,1,0:T(8,128)S(1)}, u32[]{:S(2)}, u32[]{:S(2)}) collective-permute-start(f32[4,128,128]{2,1,0:T(8,128)S(1)} %shard_map.78), channel_id=1, source_target_pairs={{0,1},{1,0},{2,3},{3,2},{4,5},{5,4},{6,7},{7,6},{8,9},{9,8},{10,11... | collective-permute-start | bytes 786440 | tf_op jit(solution)/shard_map/ppermute | solution.py:306
  34.9 8.3 %collective-permute-start.4 = (f32[4,128,128]{2,1,0:T(8,128)S(1)}, f32[4,128,128]{2,1,0:T(8,128)S(1)}, u32[]{:S(2)}, u32[]{:S(2)}) collective-permute-start(f32[4,128,128]{2,1,0:T(8,128)S(1)} %get-tuple-element.20), channel_id=1, source_target_pairs={{0,240},{16,32},{32,16},{48,64},{64,48},{80,96},{96,80},{112,128},... | collective-permute-start | bytes 786440 | tf_op jit(solution)/shard_map/ppermute | solution.py:308
  39.3 3.9 %copy-start.1 = (f32[2,2,256,256]{3,2,1,0:T(8,128)S(1)}, f32[2,2,256,256]{3,2,1,0:T(8,128)}, u32[]{:S(2)}) copy-start(f32[2,2,256,256]{3,2,1,0:T(8,128)} %param.6) | copy-start | bytes 3145732
  39.3 3.9 %copy-start.7 = (f32[2,256,256]{2,1,0:T(8,128)S(1)}, f32[2,256,256]{2,1,0:T(8,128)}, u32[]{:S(2)}) copy-start(f32[2,256,256]{2,1,0:T(8,128)} %probe.1) | copy-start | bytes 1572868
  39.3 3.9 %copy-start.8 = (s32[1,1,2,2]{3,2,1,0:T(2,128)S(1)}, s32[1,1,2,2]{3,2,1,0:T(2,128)}, u32[]{:S(2)}) copy-start(s32[1,1,2,2]{3,2,1,0:T(2,128)} %shifts.1) | copy-start | bytes 52
  57.4 22.8 %collective-permute-start.6 = (f32[4,128,512]{2,1,0:T(8,128)}, f32[4,128,512]{2,1,0:T(8,128)S(1)}, u32[]{:S(2)}, u32[]{:S(2)}) collective-permute-start(f32[4,128,512]{2,1,0:T(8,128)} %get-tuple-element.23), channel_id=1, source_target_pairs={{0,16},{16,0},{32,48},{48,32},{64,80},{80,64},{96,112},{112,96},{1... | collective-permute-start | bytes 3145736 | tf_op jit(solution)/shard_map/ppermute | solution.py:322
  62.2 13.6 %collective-permute-start.9 = (f32[4,128,128]{2,1,0:T(8,128)}, f32[4,128,128]{2,1,0:T(8,128)S(1)}, u32[]{:S(2)}, u32[]{:S(2)}) collective-permute-start(f32[4,128,128]{2,1,0:T(8,128)} %get-tuple-element.29), channel_id=1, source_target_pairs={{0,1},{1,0},{2,3},{3,2},{4,5},{5,4},{6,7},{7,6},{8,9},{9,8},{10,11... | collective-permute-start | bytes 786440 | tf_op jit(solution)/shard_map/ppermute | solution.py:324
  63.9 11.8 %collective-permute-start.10 = (f32[4,128,128]{2,1,0:T(8,128)}, f32[4,128,128]{2,1,0:T(8,128)S(1)}, u32[]{:S(2)}, u32[]{:S(2)}) collective-permute-start(f32[4,128,128]{2,1,0:T(8,128)} %get-tuple-element.30), channel_id=1, source_target_pairs={{0,15},{1,2},{2,1},{3,4},{4,3},{5,6},{6,5},{7,8},{8,7},{9,10},{10,... | collective-permute-start | bytes 786440 | tf_op jit(solution)/shard_map/ppermute | solution.py:323
  67.1 8.6 %copy-start.5 = (f32[4,128,256]{2,1,0:T(8,128)S(1)}, f32[4,128,256]{2,1,0:T(8,128)}, u32[]{:S(2)}) copy-start(f32[4,128,256]{2,1,0:T(8,128)} %get-tuple-element.28.outer) | copy-start | bytes 1572868
  67.1 19.9 %all-to-all-start = ((f32[16,2,16,256]{3,2,1,0:T(8,128)}), f32[16,2,16,256]{3,2,1,0:T(8,128)S(1)}, u32[]{:S(2)}, u32[]{:S(2)}) async-start(f32[16,2,16,256]{3,2,1,0:T(8,128)} %get-tuple-element.31), calls=%async_computation | async-start | bytes 1048576 | tf_op jit(solution)/shard_map/all_to_all | solution.py:332
  75.7 4.4 %copy-start.3 = (f32[4,256,128]{2,1,0:T(8,128)S(1)}, f32[4,256,128]{2,1,0:T(8,128)}, u32[]{:S(2)}) copy-start(f32[4,256,128]{2,1,0:T(8,128)} %get-tuple-element.24.g_a) | copy-start | bytes 1572868
  75.8 4.4 %copy-start.4 = (f32[4,256,128]{2,1,0:T(8,128)S(1)}, f32[4,256,128]{2,1,0:T(8,128)}, u32[]{:S(2)}) copy-start(f32[4,256,128]{2,1,0:T(8,128)} %get-tuple-element.25.g_b) | copy-start | bytes 1572868
  77.2 36.8 %collective-permute-start.11 = (f32[4,128,256]{2,1,0:T(8,128)}, f32[4,128,256]{2,1,0:T(8,128)S(1)}, u32[]{:S(2)}, u32[]{:S(2)}) collective-permute-start(f32[4,128,256]{2,1,0:T(8,128)} %shard_map.83), channel_id=1, source_target_pairs={{0,240},{16,32},{32,16},{48,64},{64,48},{80,96},{96,80},{112,128},... | collective-permute-start | bytes 1572872 | tf_op jit(solution)/shard_map/ppermute | solution.py:329
  80.2 33.8 %copy-start.2 = (f32[4,256,256]{2,1,0:T(8,128)S(1)}, f32[4,256,256]{2,1,0:T(8,128)}, u32[]{:S(2)}) copy-start(f32[4,256,256]{2,1,0:T(8,128)} %get-tuple-element.22.own) | copy-start | bytes 3145732
  81.9 32.1 %collective-permute-start.7 = (f32[4,256,128]{2,1,0:T(8,128)}, f32[4,256,128]{2,1,0:T(8,128)}, u32[]{:S(2)}, u32[]{:S(2)}) collective-permute-start(f32[4,256,128]{2,1,0:T(8,128)} %get-tuple-element.26), channel_id=1, source_target_pairs={{0,1},{1,0},{2,3},{3,2},{4,5},{5,4},{6,7},{7,6},{8,9},{9,8},{10,11... | collective-permute-start | bytes 1572872 | tf_op jit(solution)/shard_map/ppermute | solution.py:326
  81.9 32.1 %collective-permute-start.8 = (f32[4,256,128]{2,1,0:T(8,128)}, f32[4,256,128]{2,1,0:T(8,128)}, u32[]{:S(2)}, u32[]{:S(2)}) collective-permute-start(f32[4,256,128]{2,1,0:T(8,128)} %get-tuple-element.27), channel_id=1, source_target_pairs={{0,15},{1,2},{2,1},{3,4},{4,3},{5,6},{6,5},{7,8},{8,7},{9,10},{10,... | collective-permute-start | bytes 1572872 | tf_op jit(solution)/shard_map/ppermute | solution.py:327
where the time goes:
time: 117 us
  starting transfers between devices  36.4 us (31%)
  blocking collectives  26 us (22%)
  waiting for transfers between devices  25.8 us (22%)
  Pallas kernels  25 us (21%)
  local copies, waits for them, and re-layouts  2.4 us (2%)
    all_to_all x1, blocking collectives, body(): probe = lax.all_to_all(probe, 'col', 0, 0, tiled=True)  26 us
    pallas_call x10, Pallas kernels, call(): pl.pallas_call(kernel, out_shape=[pltpu.HBM(s, F32) if hbm else jax.Shape...  25 us
    all_to_all x1, starting transfers between devices, body(): probe = lax.all_to_all(probe, 'row', 0, 0, tiled=True)  8.58 us
    ppermute x2, waiting for transfers between devices, body(): outer = lax.ppermute(outer, 'row', FAR)  7.93 us
    ppermute x2, starting transfers between devices, body(): outer = lax.ppermute(outer, 'row', FAR)  6.25 us
    ppermute x1, waiting for transfers between devices, body(): got_a = lax.ppermute(side_a, 'col', NEAR)  5.96 us
    ppermute x1, starting transfers between devices, body(): got_b = lax.ppermute(side_b, 'col', FAR)  5.96 us
    ppermute x1, waiting for transfers between devices, body(): got_b = lax.ppermute(side_b, 'col', FAR)  5.68 us
  transfers between devices with their start and end apart: 13, of which 5 were waited for; matrix products, arithmetic and copies ran while one was open for 1% of the time, Pallas kernels for 6%

commit v1 on v0

--- a/solution.py
+++ b/solution.py
@@ -264,16 +264,23 @@
     out[1] = tall[16:32, :16]
 
 
-def call(kernel, shapes, *operands, scalars=1, scratch=(), flops=0, grant=6, hbm=False):
+def call(kernel, shapes, *operands, scalars=1, scratch=(), flops=0, grant=6, hbm=False, planes=False):
     smem = pl.BlockSpec(memory_space=pltpu.SMEM)
     vmem = pl.BlockSpec(memory_space=pltpu.VMEM)
     specs = [smem if k < scalars else vmem for k in range(len(operands))]
+    outs, grid = [vmem] * len(shapes), ()
+    if planes:
+        grid = (PARTS,)
+        plane = lambda s: pl.BlockSpec((1, *s[1:]), lambda k: (k, 0, 0))
+        specs = [smem] + [plane(x.shape) for x in operands[1:]]
+        outs = [plane(s) for s in shapes]
     size = sum(4 * math.prod(s) for s in shapes)
     return pl.pallas_call(
         kernel,
         out_shape=[pltpu.HBM(s, F32) if hbm else jax.ShapeDtypeStruct(s, F32) for s in shapes],
         in_specs=specs,
-        out_specs=[vmem] * len(shapes),
+        out_specs=outs,
+        grid=grid,
         scratch_shapes=list(scratch),
         cost_estimate=pl.CostEstimate(flops=flops, bytes_accessed=2 * size, transcendentals=0),
         compiler_params=pltpu.CompilerParams(vmem_limit_bytes=grant * 1024 * 1024),
@@ -322,12 +329,15 @@
     inner = lax.ppermute(inner, "row", NEAR)
     corner_b = lax.ppermute(corner_b, "col", FAR)
     corner_a = lax.ppermute(corner_a, "col", NEAR)
-    side_a, side_b = call(sides_kernel, [col_strip] * 2, where, side_a, side_b, inner)
+    side_a, side_b = call(sides_kernel, [col_strip] * 2, where, side_a, side_b, inner, planes=True)
     side_a = lax.ppermute(side_a, "col", NEAR)
     side_b = lax.ppermute(side_b, "col", FAR)
-    (outer,) = call(outer_kernel, [row_strip], where, outer, corner_a, corner_b)
+    (outer,) = call(outer_kernel, [row_strip], where, outer, corner_a, corner_b, planes=True)
     outer = lax.ppermute(outer, "row", FAR)
-    (result,) = call(final_kernel, [(PARTS, TILE, TILE)], where, own, inner, side_a, side_b, outer)
+    (result,) = call(
+        final_kernel, [(PARTS, TILE, TILE)], where, own, inner, side_a, side_b, outer,
+        planes=True,
+    )
 
     probe = lax.all_to_all(probe, "row", 0, 0, tiled=True)
     (probe,) = call(strip_kernel, [(16, 4, 128)], probe, scalars=0, grant=4)

time: 117 us -> 118 us (level)
  Pallas kernels: 25 us -> 27.2 us
  waiting for transfers between devices: 25.8 us -> 24 us
    pallas_call x10, Pallas kernels: 25 us -> 27.2 us  [call(): pl.pallas_call(kernel, out_shape=[pltpu.HBM(s, F32) if hbm else jax.Shape...]
    all_to_all x1, waiting for transfers between devices: 4.72 us -> 2.96 us  [body(): probe = lax.all_to_all(probe, 'row', 0, 0, tiled=True)]
  transfers between devices with their start and end apart: 13 -> 13, of which waited for: 5 -> 5; matrix products, arithmetic and copies ran while one was open for 1% -> 1% of each run, Pallas kernels for 6% -> 7%
where the time goes in v1:
time: 118 us
  starting transfers between devices  36.4 us (31%)
  Pallas kernels  27.2 us (23%)
  blocking collectives  26.7 us (23%)
  waiting for transfers between devices  24 us (20%)
  local copies, waits for them, and re-layouts  2.4 us (2%)
    pallas_call x10, Pallas kernels, call(): pl.pallas_call(kernel, out_shape=[pltpu.HBM(s, F32) if hbm else jax.Shape...  27.2 us
    all_to_all x1, blocking collectives, body(): probe = lax.all_to_all(probe, 'col', 0, 0, tiled=True)  26.7 us
    all_to_all x1, starting transfers between devices, body(): probe = lax.all_to_all(probe, 'row', 0, 0, tiled=True)  8.58 us
    ppermute x2, waiting for transfers between devices, body(): outer = lax.ppermute(outer, 'row', FAR)  7.93 us
    ppermute x2, starting transfers between devices, body(): outer = lax.ppermute(outer, 'row', FAR)  6.25 us
    ppermute x1, waiting for transfers between devices, body(): got_a = lax.ppermute(side_a, 'col', NEAR)  5.96 us
    ppermute x1, starting transfers between devices, body(): got_b = lax.ppermute(side_b, 'col', FAR)  5.96 us
    ppermute x1, waiting for transfers between devices, body(): got_b = lax.ppermute(side_b, 'col', FAR)  5.68 us
  transfers between devices with their start and end apart: 13, of which 5 were waited for; matrix products, arithmetic and copies ran while one was open for 1% of the time, Pallas kernels for 7%

profile of v1, /device:TPU:6, one launch (start us, length us, event | category | flops | bytes accessed | tf_op | source)
XLA Modules:
  0.0 117.6 jit_solution(11245838224690870794)
XLA Ops:
  0.6 0.1 pad_add_fusion.where
  0.7 1.2 %copy-done = f32[2,2,256,256]{3,2,1,0:T(8,128)S(1)} copy-done((f32[2,2,256,256]{3,2,1,0:T(8,128)S(1)}, f32[2,2,256,256]{3,2,1,0:T(8,128)}, u32[]{:S(2)}) %copy-start) | copy-done | bytes 1048600
  2.0 0.7 shard_map.77
  2.6 2.0 %collective-permute-start.1 = (f32[4,256,128]{2,1,0:T(8,128)S(1)}, f32[4,256,128]{2,1,0:T(8,128)S(1)}, u32[]{:S(2)}, u32[]{:S(2)}) collective-permute-start(f32[4,256,128]{2,1,0:T(8,128)S(1)} %get-tuple-element.18), channel_id=1, source_target_pairs={{0,1},{1,0},{2,3},{3,2},{4,5},{5,4},{6,7},{7,6},{8,9},{9,8},{10,11... | collective-permute-start | bytes 1572872 | tf_op jit(solution)/shard_map/ppermute | solution.py:306
  4.6 6.0 %collective-permute-start.2 = (f32[4,256,128]{2,1,0:T(8,128)S(1)}, f32[4,256,128]{2,1,0:T(8,128)S(1)}, u32[]{:S(2)}, u32[]{:S(2)}) collective-permute-start(f32[4,256,128]{2,1,0:T(8,128)S(1)} %get-tuple-element.19), channel_id=1, source_target_pairs={{0,15},{1,2},{2,1},{3,4},{4,3},{5,6},{6,5},{7,8},{8,7},{9,10},{10,... | collective-permute-start | bytes 1572872 | tf_op jit(solution)/shard_map/ppermute | solution.py:305
  10.6 6.0 %collective-permute-done.1.got_a = f32[4,256,128]{2,1,0:T(8,128)S(1)} collective-permute-done((f32[4,256,128]{2,1,0:T(8,128)S(1)}, f32[4,256,128]{2,1,0:T(8,128)S(1)}, u32[]{:S(2)}, u32[]{:S(2)}) %collective-permute-start.1) | collective-permute-done | bytes 524320 | tf_op jit(solution)/shard_map/ppermute | solution.py:306
  16.5 5.7 %collective-permute-done.2.got_b = f32[4,256,128]{2,1,0:T(8,128)S(1)} collective-permute-done((f32[4,256,128]{2,1,0:T(8,128)S(1)}, f32[4,256,128]{2,1,0:T(8,128)S(1)}, u32[]{:S(2)}, u32[]{:S(2)}) %collective-permute-start.2) | collective-permute-done | bytes 524320 | tf_op jit(solution)/shard_map/ppermute | solution.py:305
  22.2 0.7 shard_map.79
  22.9 0.1 collective-permute-start.5
  23.0 3.3 %collective-permute-start = (f32[4,128,256]{2,1,0:T(8,128)S(1)}, f32[4,128,256]{2,1,0:T(8,128)S(1)}, u32[]{:S(2)}, u32[]{:S(2)}) collective-permute-start(f32[4,128,256]{2,1,0:T(8,128)S(1)} %get-tuple-element.17), channel_id=1, source_target_pairs={{0,240},{16,32},{32,16},{48,64},{64,48},{80,96},{96,80},{112,128},... | collective-permute-start | bytes 1572872 | tf_op jit(solution)/shard_map/ppermute | solution.py:304
  26.3 7.9 %collective-permute-done.outer = f32[4,128,256]{2,1,0:T(8,128)S(1)} collective-permute-done((f32[4,128,256]{2,1,0:T(8,128)S(1)}, f32[4,128,256]{2,1,0:T(8,128)S(1)}, u32[]{:S(2)}, u32[]{:S(2)}) %collective-permute-start) | collective-permute-done | bytes 524320 | tf_op jit(solution)/shard_map/ppermute | solution.py:304
  34.2 0.6 shard_map.78
  34.8 0.0 copy-start.6
  34.8 0.1 collective-permute-start.3
  34.9 3.3 %collective-permute-start.4 = (f32[4,128,128]{2,1,0:T(8,128)S(1)}, f32[4,128,128]{2,1,0:T(8,128)S(1)}, u32[]{:S(2)}, u32[]{:S(2)}) collective-permute-start(f32[4,128,128]{2,1,0:T(8,128)S(1)} %get-tuple-element.20), channel_id=1, source_target_pairs={{0,240},{16,32},{32,16},{48,64},{64,48},{80,96},{96,80},{112,128},... | collective-permute-start | bytes 786440 | tf_op jit(solution)/shard_map/ppermute | solution.py:315
  38.2 0.0 copy-done.10
  38.2 1.1 fusion
  39.3 0.0 copy-start.1
  39.3 0.0 copy-start.7
  39.3 0.0 copy-start.8
  39.4 2.4 %shard_map.80.sorted_ = f32[4,256,256]{2,1,0:T(8,128)S(1)} custom-call(f32[256,256]{1,0:T(8,128)S(1)} %get-tuple-element.33.inphase, f32[256,256]{1,0:T(8,128)S(1)} %get-tuple-element.32.quadrature, f32[2,256,256]{2,1,0:T(8,128)S(1)} %bitcast.10), custom_call_target="tpu_custom_call" | custom-call | flops 300000000 | bytes 2097152 | tf_op jit(solution)/shard_map/pallas_call | solution.py:278
  41.7 0.0 collective-permute-done.3.corner_a
  41.7 1.5 %collective-permute-done.4.corner_b = f32[4,128,128]{2,1,0:T(8,128)S(1)} collective-permute-done((f32[4,128,128]{2,1,0:T(8,128)S(1)}, f32[4,128,128]{2,1,0:T(8,128)S(1)}, u32[]{:S(2)}, u32[]{:S(2)}) %collective-permute-start.4) | collective-permute-done | bytes 262176 | tf_op jit(solution)/shard_map/ppermute | solution.py:315
  43.2 0.0 collective-permute-done.5.inner
  43.2 0.0 copy-done.1
  43.2 14.2 %shard_map.81 = (f32[4,256,256]{2,1,0:T(8,128)}, f32[4,128,256]{2,1,0:T(8,128)}, f32[4,256,128]{2,1,0:T(8,128)}, f32[4,256,128]{2,1,0:T(8,128)}, f32[4,128,128]{...) custom-call(s32[4]{0:T(128)S(1)} %pad_add_fusion.where, ...), custom_call_target="tpu_custom_call" | custom-call | flops 5000000000 | bytes 9437184 | tf_op jit(solution)/shard_map/pallas_call | solution.py:278
  57.4 4.8 %collective-permute-start.6 = (f32[4,128,512]{2,1,0:T(8,128)}, f32[4,128,512]{2,1,0:T(8,128)S(1)}, u32[]{:S(2)}, u32[]{:S(2)}) collective-permute-start(f32[4,128,512]{2,1,0:T(8,128)} %get-tuple-element.23), channel_id=1, source_target_pairs={{0,16},{16,0},{32,48},{48,32},{64,80},{80,64},{96,112},{112,96},{1... | collective-permute-start | bytes 3145736 | tf_op jit(solution)/shard_map/ppermute | solution.py:329
  62.2 1.7 %collective-permute-start.9 = (f32[4,128,128]{2,1,0:T(8,128)}, f32[4,128,128]{2,1,0:T(8,128)S(1)}, u32[]{:S(2)}, u32[]{:S(2)}) collective-permute-start(f32[4,128,128]{2,1,0:T(8,128)} %get-tuple-element.29), channel_id=1, source_target_pairs={{0,1},{1,0},{2,3},{3,2},{4,5},{5,4},{6,7},{7,6},{8,9},{9,8},{10,11... | collective-permute-start | bytes 786440 | tf_op jit(solution)/shard_map/ppermute | solution.py:331
  63.9 3.2 %collective-permute-start.10 = (f32[4,128,128]{2,1,0:T(8,128)}, f32[4,128,128]{2,1,0:T(8,128)S(1)}, u32[]{:S(2)}, u32[]{:S(2)}) collective-permute-start(f32[4,128,128]{2,1,0:T(8,128)} %get-tuple-element.30), channel_id=1, source_target_pairs={{0,15},{1,2},{2,1},{3,4},{4,3},{5,6},{6,5},{7,8},{8,7},{9,10},{10,... | collective-permute-start | bytes 786440 | tf_op jit(solution)/shard_map/ppermute | solution.py:330
  67.1 8.6 %all-to-all-start = ((f32[16,2,16,256]{3,2,1,0:T(8,128)}), f32[16,2,16,256]{3,2,1,0:T(8,128)S(1)}, u32[]{:S(2)}, u32[]{:S(2)}) async-start(f32[16,2,16,256]{3,2,1,0:T(8,128)} %get-tuple-element.31), calls=%async_computation | async-start | bytes 1048576 | tf_op jit(solution)/shard_map/all_to_all | solution.py:342
  75.7 0.0 collective-permute-done.9.corner_a
  75.7 0.0 collective-permute-done.10.corner_b
  75.8 2.0 %shard_map.83 = f32[4,128,256]{2,1,0:T(8,128)} custom-call(s32[4]{0:T(128)S(1)} %pad_add_fusion.where, f32[4,128,256]{2,1,0:T(8,128)S(1)} %copy-done.5, f32[4,128,128]{2,1,0:T(8,128)S(1)} %collective-permute-done.9.corner_a, f32[4,128,128]{2,1,0:T(8,128)S(1)} %collective-permute-done.10.corner_b), custom_call_target="tpu_custom_call" | custom-call | bytes 1048576 | tf_op jit(solution)/shard_map/pallas_call | solution.py:278
  77.8 3.0 %collective-permute-start.11 = (f32[4,128,256]{2,1,0:T(8,128)}, f32[4,128,256]{2,1,0:T(8,128)S(1)}, u32[]{:S(2)}, u32[]{:S(2)}) collective-permute-start(f32[4,128,256]{2,1,0:T(8,128)} %shard_map.83), channel_id=1, source_target_pairs={{0,240},{16,32},{32,16},{48,64},{64,48},{80,96},{96,80},{112,128},... | collective-permute-start | bytes 1572872 | tf_op jit(solution)/shard_map/ppermute | solution.py:336
  80.7 0.0 collective-permute-done.6.inner
  80.7 0.0 copy-done.3
  80.8 0.0 copy-start.2
  80.8 2.2 %shard_map.82 = (f32[4,256,128]{2,1,0:T(8,128)}, f32[4,256,128]{2,1,0:T(8,128)}) custom-call(s32[4]{0:T(128)S(1)} %pad_add_fusion.where, f32[4,256,128]{2,1,0:T(8,128)S(1)} %copy-done.3, f32[4,256,128]{2,1,0:T(8,128)S(1)} %copy-done.4, f32[4,128,512]{2,1,0:T(8,128)S(1)} %collective-permute-done.6.inner), custom_call_target="tpu_custom_call" | custom-call | bytes 2097152 | tf_op jit(solution)/shard_map/pallas_call | solution.py:278
  83.0 0.0 collective-permute-start.7
  83.0 0.4 collective-permute-start.8
  83.4 3.0 %all-to-all-done.got = f32[16,2,16,256]{3,2,1,0:T(8,128)S(1)} async-done(((f32[16,2,16,256]{3,2,1,0:T(8,128)}), f32[16,2,16,256]{3,2,1,0:T(8,128)S(1)}, u32[]{:S(2)}, u32[]{:S(2)}) %all-to-all-start) | async-done | bytes 524320 | tf_op jit(solution)/shard_map/all_to_all | solution.py:342
  86.3 0.2 shard_map.85
  86.6 26.7 %all_to_all.10.got = f32[16,4,128]{2,1,0:T(4,128)S(1)} all-to-all(f32[16,4,128]{2,1,0:T(4,128)S(1)} %shard_map.85), channel_id=1, replica_groups=mesh['row'=16,'col'=16] {'col'}, dimensions={0} | all-to-all | bytes 65536 | tf_op jit(solution)/shard_map/all_to_all | solution.py:344
  113.2 0.8 shard_map.86
  114.0 0.0 collective-permute-done.11.outer
  114.0 0.0 collective-permute-done.7.side_a
  114.0 0.0 collective-permute-done.8.side_b
  114.0 3.6 %shard_map.84 = f32[4,256,256]{2,1,0:T(8,128)} custom-call(s32[4]{0:T(128)S(1)} %pad_add_fusion.where, f32[4,256,256]{2,1,0:T(8,128)S(1)} %copy-done.2, f32[4,128,512]{2,1,0:T(8,128)S(1)} %collective-permute-done.6.inner, f32[4,256,128]{2,1,0:T(8,128)} %collective-permute-done.7.side_a, f32[4,256,128]{2,1,0:T(8,128)} %collective-permute-done.8.side_b, ...), custom_call_target="tpu_custom_call" | custom-call | bytes 2097152 | tf_op jit(solution)/shard_map/pallas_call | solution.py:278
  (13 shorter events, 0.0 us)
Async XLA Ops:
  0.7 1.2 %copy-start = (f32[2,2,256,256]{3,2,1,0:T(8,128)S(1)}, f32[2,2,256,256]{3,2,1,0:T(8,128)}, u32[]{:S(2)}) copy-start(f32[2,2,256,256]{3,2,1,0:T(8,128)} %param.6) | copy-start | bytes 3145732
  2.6 13.9 %collective-permute-start.1 = (f32[4,256,128]{2,1,0:T(8,128)S(1)}, f32[4,256,128]{2,1,0:T(8,128)S(1)}, u32[]{:S(2)}, u32[]{:S(2)}) collective-permute-start(f32[4,256,128]{2,1,0:T(8,128)S(1)} %get-tuple-element.18), channel_id=1, source_target_pairs={{0,1},{1,0},{2,3},{3,2},{4,5},{5,4},{6,7},{7,6},{8,9},{9,8},{10,11... | collective-permute-start | bytes 1572872 | tf_op jit(solution)/shard_map/ppermute | solution.py:306
  4.6 17.6 %collective-permute-start.2 = (f32[4,256,128]{2,1,0:T(8,128)S(1)}, f32[4,256,128]{2,1,0:T(8,128)S(1)}, u32[]{:S(2)}, u32[]{:S(2)}) collective-permute-start(f32[4,256,128]{2,1,0:T(8,128)S(1)} %get-tuple-element.19), channel_id=1, source_target_pairs={{0,15},{1,2},{2,1},{3,4},{4,3},{5,6},{6,5},{7,8},{8,7},{9,10},{10,... | collective-permute-start | bytes 1572872 | tf_op jit(solution)/shard_map/ppermute | solution.py:305
  22.2 16.0 %copy-start.10 = (f32[256,256]{1,0:T(8,128)S(1)}, f32[256,256]{1,0:T(8,128)}, u32[]{:S(2)}) copy-start(f32[256,256]{1,0:T(8,128)} %param.8) | copy-start | bytes 786436
  22.9 20.3 %collective-permute-start.5 = (f32[4,128,512]{2,1,0:T(8,128)S(1)}, f32[4,128,512]{2,1,0:T(8,128)S(1)}, u32[]{:S(2)}, u32[]{:S(2)}) collective-permute-start(f32[4,128,512]{2,1,0:T(8,128)S(1)} %get-tuple-element.21), channel_id=1, source_target_pairs={{0,16},{16,0},{32,48},{48,32},{64,80},{80,64},{96,112},{112,96},{1... | collective-permute-start | bytes 3145736 | tf_op jit(solution)/shard_map/ppermute | solution.py:316
  23.0 11.2 %collective-permute-start = (f32[4,128,256]{2,1,0:T(8,128)S(1)}, f32[4,128,256]{2,1,0:T(8,128)S(1)}, u32[]{:S(2)}, u32[]{:S(2)}) collective-permute-start(f32[4,128,256]{2,1,0:T(8,128)S(1)} %get-tuple-element.17), channel_id=1, source_target_pairs={{0,240},{16,32},{32,16},{48,64},{64,48},{80,96},{96,80},{112,128},... | collective-permute-start | bytes 1572872 | tf_op jit(solution)/shard_map/ppermute | solution.py:304
  34.2 9.0 %copy-start.9 = (bf16[8,256,256]{2,1,0:T(8,128)(2,1)S(1)}, bf16[8,256,256]{2,1,0:T(8,128)(2,1)}, u32[]{:S(2)}) copy-start(bf16[8,256,256]{2,1,0:T(8,128)(2,1)} %constant.28.clone.tables) | copy-start | bytes 3145732
  34.8 4.5 %copy-start.6 = (f32[1,1,2,256,256]{4,3,2,1,0:T(8,128)S(1)}, f32[1,1,2,256,256]{4,3,2,1,0:T(8,128)}, u32[]{:S(2)}) copy-start(f32[1,1,2,256,256]{4,3,2,1,0:T(8,128)} %param.9) | copy-start | bytes 1572868
  34.8 6.9 %collective-permute-start.3 = (f32[4,128,128]{2,1,0:T(8,128)S(1)}, f32[4,128,128]{2,1,0:T(8,128)S(1)}, u32[]{:S(2)}, u32[]{:S(2)}) collective-permute-start(f32[4,128,128]{2,1,0:T(8,128)S(1)} %shard_map.78), channel_id=1, source_target_pairs={{0,1},{1,0},{2,3},{3,2},{4,5},{5,4},{6,7},{7,6},{8,9},{9,8},{10,11... | collective-permute-start | bytes 786440 | tf_op jit(solution)/shard_map/ppermute | solution.py:313
  34.9 8.3 %collective-permute-start.4 = (f32[4,128,128]{2,1,0:T(8,128)S(1)}, f32[4,128,128]{2,1,0:T(8,128)S(1)}, u32[]{:S(2)}, u32[]{:S(2)}) collective-permute-start(f32[4,128,128]{2,1,0:T(8,128)S(1)} %get-tuple-element.20), channel_id=1, source_target_pairs={{0,240},{16,32},{32,16},{48,64},{64,48},{80,96},{96,80},{112,128},... | collective-permute-start | bytes 786440 | tf_op jit(solution)/shard_map/ppermute | solution.py:315
  39.3 3.9 %copy-start.1 = (f32[2,2,256,256]{3,2,1,0:T(8,128)S(1)}, f32[2,2,256,256]{3,2,1,0:T(8,128)}, u32[]{:S(2)}) copy-start(f32[2,2,256,256]{3,2,1,0:T(8,128)} %param.6) | copy-start | bytes 3145732
  39.3 3.9 %copy-start.7 = (f32[2,256,256]{2,1,0:T(8,128)S(1)}, f32[2,256,256]{2,1,0:T(8,128)}, u32[]{:S(2)}) copy-start(f32[2,256,256]{2,1,0:T(8,128)} %probe.1) | copy-start | bytes 1572868
  39.3 3.9 %copy-start.8 = (s32[1,1,2,2]{3,2,1,0:T(2,128)S(1)}, s32[1,1,2,2]{3,2,1,0:T(2,128)}, u32[]{:S(2)}) copy-start(s32[1,1,2,2]{3,2,1,0:T(2,128)} %shifts.1) | copy-start | bytes 52
  57.4 23.4 %collective-permute-start.6 = (f32[4,128,512]{2,1,0:T(8,128)}, f32[4,128,512]{2,1,0:T(8,128)S(1)}, u32[]{:S(2)}, u32[]{:S(2)}) collective-permute-start(f32[4,128,512]{2,1,0:T(8,128)} %get-tuple-element.23), channel_id=1, source_target_pairs={{0,16},{16,0},{32,48},{48,32},{64,80},{80,64},{96,112},{112,96},{1... | collective-permute-start | bytes 3145736 | tf_op jit(solution)/shard_map/ppermute | solution.py:329
  62.2 13.6 %collective-permute-start.9 = (f32[4,128,128]{2,1,0:T(8,128)}, f32[4,128,128]{2,1,0:T(8,128)S(1)}, u32[]{:S(2)}, u32[]{:S(2)}) collective-permute-start(f32[4,128,128]{2,1,0:T(8,128)} %get-tuple-element.29), channel_id=1, source_target_pairs={{0,1},{1,0},{2,3},{3,2},{4,5},{5,4},{6,7},{7,6},{8,9},{9,8},{10,11... | collective-permute-start | bytes 786440 | tf_op jit(solution)/shard_map/ppermute | solution.py:331
  63.9 11.8 %collective-permute-start.10 = (f32[4,128,128]{2,1,0:T(8,128)}, f32[4,128,128]{2,1,0:T(8,128)S(1)}, u32[]{:S(2)}, u32[]{:S(2)}) collective-permute-start(f32[4,128,128]{2,1,0:T(8,128)} %get-tuple-element.30), channel_id=1, source_target_pairs={{0,15},{1,2},{2,1},{3,4},{4,3},{5,6},{6,5},{7,8},{8,7},{9,10},{10,... | collective-permute-start | bytes 786440 | tf_op jit(solution)/shard_map/ppermute | solution.py:330
  67.1 8.6 %copy-start.5 = (f32[4,128,256]{2,1,0:T(8,128)S(1)}, f32[4,128,256]{2,1,0:T(8,128)}, u32[]{:S(2)}) copy-start(f32[4,128,256]{2,1,0:T(8,128)} %get-tuple-element.28.outer) | copy-start | bytes 1572868
  67.1 19.2 %all-to-all-start = ((f32[16,2,16,256]{3,2,1,0:T(8,128)}), f32[16,2,16,256]{3,2,1,0:T(8,128)S(1)}, u32[]{:S(2)}, u32[]{:S(2)}) async-start(f32[16,2,16,256]{3,2,1,0:T(8,128)} %get-tuple-element.31), calls=%async_computation | async-start | bytes 1048576 | tf_op jit(solution)/shard_map/all_to_all | solution.py:342
  75.7 5.0 %copy-start.3 = (f32[4,256,128]{2,1,0:T(8,128)S(1)}, f32[4,256,128]{2,1,0:T(8,128)}, u32[]{:S(2)}) copy-start(f32[4,256,128]{2,1,0:T(8,128)} %get-tuple-element.24.g_a) | copy-start | bytes 1572868
  75.8 5.0 %copy-start.4 = (f32[4,256,128]{2,1,0:T(8,128)S(1)}, f32[4,256,128]{2,1,0:T(8,128)}, u32[]{:S(2)}) copy-start(f32[4,256,128]{2,1,0:T(8,128)} %get-tuple-element.25.g_b) | copy-start | bytes 1572868
  77.8 36.2 %collective-permute-start.11 = (f32[4,128,256]{2,1,0:T(8,128)}, f32[4,128,256]{2,1,0:T(8,128)S(1)}, u32[]{:S(2)}, u32[]{:S(2)}) collective-permute-start(f32[4,128,256]{2,1,0:T(8,128)} %shard_map.83), channel_id=1, source_target_pairs={{0,240},{16,32},{32,16},{48,64},{64,48},{80,96},{96,80},{112,128},... | collective-permute-start | bytes 1572872 | tf_op jit(solution)/shard_map/ppermute | solution.py:336
  80.8 33.3 %copy-start.2 = (f32[4,256,256]{2,1,0:T(8,128)S(1)}, f32[4,256,256]{2,1,0:T(8,128)}, u32[]{:S(2)}) copy-start(f32[4,256,256]{2,1,0:T(8,128)} %get-tuple-element.22.own) | copy-start | bytes 3145732
  83.0 31.0 %collective-permute-start.7 = (f32[4,256,128]{2,1,0:T(8,128)}, f32[4,256,128]{2,1,0:T(8,128)}, u32[]{:S(2)}, u32[]{:S(2)}) collective-permute-start(f32[4,256,128]{2,1,0:T(8,128)} %get-tuple-element.26), channel_id=1, source_target_pairs={{0,1},{1,0},{2,3},{3,2},{4,5},{5,4},{6,7},{7,6},{8,9},{9,8},{10,11... | collective-permute-start | bytes 1572872 | tf_op jit(solution)/shard_map/ppermute | solution.py:333
  83.0 31.0 %collective-permute-start.8 = (f32[4,256,128]{2,1,0:T(8,128)}, f32[4,256,128]{2,1,0:T(8,128)}, u32[]{:S(2)}, u32[]{:S(2)}) collective-permute-start(f32[4,256,128]{2,1,0:T(8,128)} %get-tuple-element.27), channel_id=1, source_target_pairs={{0,15},{1,2},{2,1},{3,4},{4,3},{5,6},{6,5},{7,8},{8,7},{9,10},{10,... | collective-permute-start | bytes 1572872 | tf_op jit(solution)/shard_map/ppermute | solution.py:334
